TPU v7x, 32 devices: a whole 2x2x4 slice. The times are simulated.
32 devices in a mesh: groups: 2 (over x), samples: 16 (over z, y, core).
Axes of the slice: x: 2, y: 2, z: 4, core: 2. Of those that a mesh axis runs over, the one named last changes fastest.
Arguments:
- terms: float32 [1048576, 64], P(('groups', 'samples')), parts along dimension 0
- coefficients: float32 [64, 256], replicated, may hold values from -1.5 to 1.5
- counts: int32 [512], P('groups'), parts along dimension 0, may hold values from 1 to 4095, as said below
- labels: int32 [1048576], P(('groups', 'samples')), parts along dimension 0, may hold values from 0 to 255, as said below
- f_start: float32 [512], P('groups'), parts along dimension 0, may hold values from -8 to 8
Outputs:
- free: float32 [512], P('groups'), parts along dimension 0
- intersection: float32 [512, 256], P(('groups', 'samples')), parts along dimension 0
- anchor_mix: float32 [512, 256], P(('groups', 'samples')), parts along dimension 0
- term_means: float32 [512, 64], P(('groups', 'samples')), parts along dimension 0
There are 2 independent parts, one for each index of `groups`. A program takes and returns all parts, laid end to end along the dimension named above; an argument that names none is the same for every part. Nothing has to cross between parts.
Inputs may be any that keep to these rules, and one draw needn't show every extreme that they name: counts sum to 524288. `labels`: exactly counts[k] snapshots carry the label k.
All inputs are finite; a program needn't handle non-finite values.
Results may differ from a plain program's by a relative error of at most 0.0003.
Values sent between devices are 32-bit elements; how exact they have to be, the bound alone decides.
A program may use at most 128 MiB of HBM per device.

v0:
```python
import jax
import jax.numpy as jnp
from jax import lax
from jax.sharding import PartitionSpec as P

ITERS = 4


def energies(block, coefficients):
    return jnp.dot(
        block, coefficients, precision=lax.Precision.HIGHEST, preferred_element_type=jnp.float32
    )


def denominator(energy, free_now, log_counts):
    shifted = log_counts[None, :] + free_now[None, :] - energy
    top = jnp.max(shifted, axis=1, keepdims=True)
    return top[:, 0] + jnp.log(jnp.sum(jnp.exp(shifted - top), axis=1))


def local(terms, coefficients, counts, labels, f_start):
    rows = terms.shape[0]
    states = coefficients.shape[1]
    block_rows = min(4096, rows)
    blocks = terms.reshape(rows // block_rows, block_rows, terms.shape[1])
    label_blocks = labels.reshape(rows // block_rows, block_rows)
    log_counts = jnp.log(counts.astype(jnp.float32))
    scaled_counts = counts.astype(jnp.float32)
    free_now = f_start
    for step in range(ITERS):

        def accumulate(carry, block):
            peak, total = carry
            energy = energies(block, coefficients)
            denom = denominator(energy, free_now, log_counts)
            logw = -energy - denom[:, None]
            new_peak = jnp.maximum(peak, jnp.max(logw, axis=0))
            total = total * jnp.exp(peak - new_peak) + jnp.sum(
                jnp.exp(logw - new_peak[None, :]), axis=0
            )
            return ((new_peak, total), None)

        init = (jnp.full((states,), -1e30, jnp.float32), jnp.zeros((states,), jnp.float32))
        (peak, total), _ = lax.scan(accumulate, init, blocks)
        highest = lax.pmax(peak, "samples")
        total = lax.psum(total * jnp.exp(peak - highest), "samples")
        peak = highest
        updated = -(peak + jnp.log(total))
        free_now = updated - updated[0]
    state_ids = jnp.arange(states, dtype=jnp.int32)

    def diagnose(carry, pair):
        over, anchor, term_sum, weight_sum = carry
        block, label_block = pair
        energy = energies(block, coefficients)
        denom = denominator(energy, free_now, log_counts)
        weight = jnp.exp(free_now[None, :] - energy - denom[:, None])
        over = over + jnp.dot(
            weight.T,
            weight * scaled_counts[None, :],
            precision=lax.Precision.HIGHEST,
            preferred_element_type=jnp.float32,
        )
        onehot = (label_block[:, None] == state_ids[None, :]).astype(jnp.float32)
        anchor = anchor + jnp.dot(
            onehot.T, weight, precision=lax.Precision.HIGHEST, preferred_element_type=jnp.float32
        )
        term_sum = term_sum + jnp.dot(
            weight.T, block, precision=lax.Precision.HIGHEST, preferred_element_type=jnp.float32
        )
        weight_sum = weight_sum + jnp.sum(weight, axis=0)
        return ((over, anchor, term_sum, weight_sum), None)

    init = (
        jnp.zeros((states, states), jnp.float32),
        jnp.zeros((states, states), jnp.float32),
        jnp.zeros((states, terms.shape[1]), jnp.float32),
        jnp.zeros((states,), jnp.float32),
    )
    (over, anchor, term_sum, weight_sum), _ = lax.scan(diagnose, init, (blocks, label_blocks))
    over, anchor, term_sum, weight_sum = lax.psum((over, anchor, term_sum, weight_sum), "samples")
    owned = states // lax.axis_size("samples")
    first_row = lax.axis_index("samples") * owned
    over = lax.dynamic_slice_in_dim(over, first_row, owned, 0)
    anchor = lax.dynamic_slice_in_dim(anchor, first_row, owned, 0)
    term_sum = lax.dynamic_slice_in_dim(term_sum, first_row, owned, 0)
    weight_sum = lax.dynamic_slice_in_dim(weight_sum, first_row, owned, 0)
    return (free_now, over, anchor, term_sum / weight_sum[:, None])


def solution(mesh):
    return jax.shard_map(
        local,
        mesh=mesh,
        in_specs=(
            P(("groups", "samples"), None),
            P(),
            P("groups"),
            P(("groups", "samples")),
            P("groups"),
        ),
        out_specs=(
            P("groups"),
            P(("groups", "samples"), None),
            P(("groups", "samples"), None),
            P(("groups", "samples"), None),
        ),
        check_vma=False,
    )
```

profile of v0, /device:TPU:0, one launch (start us, length us, event | category | flops | bytes accessed | tf_op | source)
XLA Modules:
  0.0 897.7 jit_solution(15325472563780318898)
XLA Ops:
  7.4 12.3 %copy.9 = f32[32768,64]{1,0:T(8,128)} copy(f32[32768,64]{0,1:T(8,128)} %param.15) | data formatting | bytes 16777216 | tf_op args[0]
  19.7 84.8 %while.79 = (s32[]{:T(128)}, f32[256]{0:T(256)S(1)}, f32[256]{0:T(256)S(1)}, f32[8,4096,64]{2,1,0:T(8,128)}, f32[64,256]{1,0:T(8,128)S(1)}, /*index=5*/f32[1,256]{1,0:T(1,128)S(1)}, s32[]{:T(128)}, s32[]{:T(128)}) while((s32[]{:T(128)}, f32[256]{0:T(256)S(1)}, f32[256]{0:T(256)S(1)}, f32[8,4096,64]{2,1,0:T(8,128)}, ...), condition=%wide.region_5.6_spmd.clone, body=%wide.region_0.5_spmd.clone.sunk | while | flops 817886464 | bytes 35864184 | solution.py:44
  19.7 5.2 subtract_reduce_fusion.10
  30.3 5.2 subtract_reduce_fusion.10
  51.5 5.2 subtract_reduce_fusion.10
  62.1 5.2 subtract_reduce_fusion.10
  83.3 5.2 subtract_reduce_fusion.10
  93.9 5.2 subtract_reduce_fusion.10
  104.5 35.0 %pmax.28 = f32[256]{0:T(256)S(1)} all-reduce(f32[256]{0:T(256)S(1)} %get-tuple-element.470), channel_id=1, replica_groups=mesh['groups'=2,'samples'=16] {'samples'}, use_global_device_ids=true, to_apply=%region_6.7 | all-reduce | flops 256 | bytes 2048 | tf_op jit(solution)/shard_map/pmax | solution.py:45
  139.4 29.5 %psum.56 = f32[256]{0:T(256)S(1)} all-reduce(f32[256]{0:T(256)S(1)} %exponential_multiply_fusion.3), channel_id=1, replica_groups=mesh['groups'=2,'samples'=16] {'samples'}, use_global_device_ids=true, to_apply=%region_7.8 | all-reduce | flops 256 | bytes 2048 | tf_op jit(solution)/shard_map/psum | solution.py:46
  170.0 84.8 %while.80 = (s32[]{:T(128)}, f32[256]{0:T(256)S(1)}, f32[256]{0:T(256)S(1)}, f32[8,4096,64]{2,1,0:T(8,128)}, f32[64,256]{1,0:T(8,128)S(1)}, /*index=5*/f32[1,256]{1,0:T(1,128)S(1)}, s32[]{:T(128)}, s32[]{:T(128)}) while((s32[]{:T(128)}, f32[256]{0:T(256)S(1)}, f32[256]{0:T(256)S(1)}, f32[8,4096,64]{2,1,0:T(8,128)}, ...), condition=%wide.region_13.14_spmd.clone, body=%wide.region_8.13_spmd.clone.sunk | while | flops 817886464 | bytes 35864184 | solution.py:44
  191.2 5.2 subtract_reduce_fusion.11
  233.6 5.2 subtract_reduce_fusion.11
  254.8 29.5 %pmax.29 = f32[256]{0:T(256)S(1)} all-reduce(f32[256]{0:T(256)S(1)} %get-tuple-element.472), channel_id=1, replica_groups=mesh['groups'=2,'samples'=16] {'samples'}, use_global_device_ids=true, to_apply=%region_14.15 | all-reduce | flops 256 | bytes 2048 | tf_op jit(solution)/shard_map/pmax | solution.py:45
  284.3 29.7 %psum.57 = f32[256]{0:T(256)S(1)} all-reduce(f32[256]{0:T(256)S(1)} %exponential_multiply_fusion.2), channel_id=1, replica_groups=mesh['groups'=2,'samples'=16] {'samples'}, use_global_device_ids=true, to_apply=%region_15.16 | all-reduce | flops 256 | bytes 2048 | tf_op jit(solution)/shard_map/psum | solution.py:46
  315.1 84.8 %while.81 = (s32[]{:T(128)}, f32[256]{0:T(256)S(1)}, f32[256]{0:T(256)S(1)}, f32[8,4096,64]{2,1,0:T(8,128)}, f32[64,256]{1,0:T(8,128)S(1)}, /*index=5*/f32[1,256]{1,0:T(1,128)S(1)}, s32[]{:T(128)}, s32[]{:T(128)}) while((s32[]{:T(128)}, f32[256]{0:T(256)S(1)}, f32[256]{0:T(256)S(1)}, f32[8,4096,64]{2,1,0:T(8,128)}, ...), condition=%wide.region_21.22_spmd.clone, body=%wide.region_16.21_spmd.clone.sunk | while | flops 817886464 | bytes 35864184 | solution.py:44
  399.9 29.5 %pmax.30 = f32[256]{0:T(256)S(1)} all-reduce(f32[256]{0:T(256)S(1)} %get-tuple-element.474), channel_id=1, replica_groups=mesh['groups'=2,'samples'=16] {'samples'}, use_global_device_ids=true, to_apply=%region_22.23 | all-reduce | flops 256 | bytes 2048 | tf_op jit(solution)/shard_map/pmax | solution.py:45
  429.4 29.5 %psum.58 = f32[256]{0:T(256)S(1)} all-reduce(f32[256]{0:T(256)S(1)} %exponential_multiply_fusion.1), channel_id=1, replica_groups=mesh['groups'=2,'samples'=16] {'samples'}, use_global_device_ids=true, to_apply=%region_23.24 | all-reduce | flops 256 | bytes 2048 | tf_op jit(solution)/shard_map/psum | solution.py:46
  460.1 84.9 %while.82 = (s32[]{:T(128)}, f32[256]{0:T(256)S(1)}, f32[256]{0:T(256)S(1)}, f32[8,4096,64]{2,1,0:T(8,128)}, f32[64,256]{1,0:T(8,128)S(1)}, /*index=5*/f32[1,256]{1,0:T(1,128)S(1)}, s32[]{:T(128)}, s32[]{:T(128)}) while((s32[]{:T(128)}, f32[256]{0:T(256)S(1)}, f32[256]{0:T(256)S(1)}, f32[8,4096,64]{2,1,0:T(8,128)}, ...), condition=%wide.region_29.30_spmd.clone, body=%wide.region_24.29_spmd.clone.sunk | while | flops 817886464 | bytes 35864184 | solution.py:44
  460.1 5.2 subtract_reduce_fusion.13
  470.7 5.2 subtract_reduce_fusion.13
  481.3 5.2 subtract_reduce_fusion.13
  491.9 5.2 subtract_reduce_fusion.13
  502.5 5.2 subtract_reduce_fusion.13
  513.1 5.2 subtract_reduce_fusion.13
  523.7 5.2 subtract_reduce_fusion.13
  534.3 5.2 subtract_reduce_fusion.13
  544.9 29.5 %pmax.31 = f32[256]{0:T(256)S(1)} all-reduce(f32[256]{0:T(256)S(1)} %get-tuple-element.476), channel_id=1, replica_groups=mesh['groups'=2,'samples'=16] {'samples'}, use_global_device_ids=true, to_apply=%region_30.31 | all-reduce | flops 256 | bytes 2048 | tf_op jit(solution)/shard_map/pmax | solution.py:45
  574.4 29.5 %psum.59 = f32[256]{0:T(256)S(1)} all-reduce(f32[256]{0:T(256)S(1)} %exponential_multiply_fusion), channel_id=1, replica_groups=mesh['groups'=2,'samples'=16] {'samples'}, use_global_device_ids=true, to_apply=%region_31.32 | all-reduce | flops 256 | bytes 2048 | tf_op jit(solution)/shard_map/psum | solution.py:46
  605.2 192.2 %while.83 = (s32[]{:T(128)}, f32[256,256]{1,0:T(8,128)S(1)}, f32[256,256]{1,0:T(8,128)S(1)}, f32[256,64]{0,1:T(8,128)S(1)}, f32[256]{0:T(256)S(1)}, /*index=5*/f...) while((s32[]{:T(128)}, f32[256,256]{1,0:T(8,128)S(1)}, ...), condition=%wide.region_36.37_spmd.clone, body=%wide.region_32.36_spmd.clone.sunk | while | flops 8073277952 | bytes 64385216 | solution.py:80
  605.4 5.3 subtract_reduce_fusion.14
  613.5 7.2 fusion.106
  629.4 5.3 subtract_reduce_fusion.14
  637.5 7.2 fusion.106
  653.4 5.3 subtract_reduce_fusion.14
  661.5 7.2 fusion.106
  677.4 5.3 subtract_reduce_fusion.14
  685.5 7.2 fusion.106
  701.4 5.3 subtract_reduce_fusion.14
  709.5 7.2 fusion.106
  725.4 5.3 subtract_reduce_fusion.14
  733.5 7.2 fusion.106
  749.4 5.3 subtract_reduce_fusion.14
  757.5 7.2 fusion.106
  773.4 5.3 subtract_reduce_fusion.14
  781.5 7.2 fusion.106
  798.2 29.7 %psum.63 = f32[256]{0:T(256)S(1)} all-reduce(f32[256]{0:T(256)S(1)} %get-tuple-element.481), channel_id=1, replica_groups=mesh['groups'=2,'samples'=16] {'samples'}, use_global_device_ids=true, to_apply=%region_40.41 | all-reduce | flops 256 | bytes 2048 | tf_op jit(solution)/shard_map/psum | solution.py:81
  828.0 59.8 %all-reduce.3.cloned.1.call-done = (f32[256,256]{1,0:T(8,128)}, f32[256,256]{1,0:T(8,128)}, f32[256,64]{1,0:T(8,128)}) async-done(((f32[256,256]{1,0:T(8,128)}, f32[256,256]{1,0:T(8,128)}, f32[256,64]{1,0:T(8,128)}), (f32[256,256]{1,0:T(8,128)}, f32[256,256]{1,0:T(8,128)}, f32[256,64]{1,0:T(8,128)})) %all-reduce.3.cloned.1.call-update) | async-done | bytes 589840 | tf_op jit(solution)/shard_map/psum | solution.py:81
  (443 shorter events, 353.1 us)
Async XLA Ops:
  7.2 880.6 %all-reduce.3.cloned.1.call-start = ((), (), s32[]{:S(2)}) async-start(), calls=%async_computation | async-start | bytes 1310720 | tf_op jit(solution)/shard_map/psum | solution.py:81
  7.3 12.3 %copy-start.11 = (s32[256]{0:T(256)S(1)}, s32[256]{0:T(256)}, u32[]{:S(2)}) copy-start(s32[256]{0:T(256)} %param.17) | copy-start | bytes 3076
  7.3 12.3 %copy-start.12 = (f32[256]{0:T(256)S(1)}, f32[256]{0:T(256)}, u32[]{:S(2)}) copy-start(f32[256]{0:T(256)} %param.19) | copy-start | bytes 3076
  7.3 12.3 %copy-start.6 = (f32[64,256]{1,0:T(8,128)S(1)}, f32[64,256]{1,0:T(8,128)}, u32[]{:S(2)}) copy-start(f32[64,256]{1,0:T(8,128)} %param.16) | copy-start | bytes 196612
  24.8 1.9 copy-start.2
  35.4 1.9 copy-start.2
  46.0 1.9 copy-start.2
  56.6 1.9 copy-start.2
  67.2 1.9 copy-start.2
  77.8 1.9 copy-start.2
  88.4 1.9 copy-start.2
  99.0 1.9 copy-start.2
  175.2 1.9 copy-start.3
  185.8 1.9 copy-start.3
  196.4 1.9 copy-start.3
  207.0 1.9 copy-start.3
  217.6 1.9 copy-start.3
  228.2 1.9 copy-start.3
  238.8 1.9 copy-start.3
  249.4 1.9 copy-start.3
  320.3 1.9 copy-start.4
  330.9 1.9 copy-start.4
  341.5 1.9 copy-start.4
  352.1 1.9 copy-start.4
  362.7 1.9 copy-start.4
  373.3 1.9 copy-start.4
  383.9 1.9 copy-start.4
  394.5 1.9 copy-start.4
  460.1 145.0 %copy-start.9 = (s32[32768]{0:T(1024)S(1)}, s32[32768]{0:T(1024)}, u32[]{:S(2)}) copy-start(s32[32768]{0:T(1024)} %param.18) | copy-start | bytes 393220
  465.3 1.9 copy-start.5
  475.9 1.9 copy-start.5
  486.5 1.9 copy-start.5
  497.1 1.9 copy-start.5
  507.7 1.9 copy-start.5
  518.3 1.9 copy-start.5
  528.9 1.9 copy-start.5
  539.5 1.9 copy-start.5
  613.5 7.3 copy-start.1
  637.5 7.3 copy-start.1
  658.7 1.9 copy-start
  661.5 7.3 copy-start.1
  682.7 1.9 copy-start
  685.5 7.3 copy-start.1
  709.5 7.3 copy-start.1
  733.5 7.3 copy-start.1
  757.5 7.3 copy-start.1
  781.5 7.3 copy-start.1
  797.4 93.1 %copy-start.10 = (f32[256]{0:T(256)}, f32[256]{0:T(256)S(1)}, u32[]{:S(2)}) copy-start(f32[256]{0:T(256)S(1)} %get-tuple-element.1079) | copy-start | bytes 3076
  (8 other events, 13.2 us)
Sparse Core Ops, SparseCore 0:
  798.4 89.3 all-reduce.2
where the time goes:
time: 908 us; the launch traced here: 898 us
  matrix products  335 us (37%)
  blocking collectives  271 us (30%)
  other arithmetic  176 us (19%)
  waiting for transfers between devices  59.8 us (7%)
  local copies, waits for them, and re-layouts  38.3 us (4%)
  between operations  14.7 us (2%)
    dot_general x40, matrix products, energies(): jnp.dot(block, coefficients, precision=lax.Precision.HIGHEST, preferred_e...  208 us
    pmax x4, blocking collectives, local(): highest = lax.pmax(peak, 'samples')  123 us
    psum x4, blocking collectives, local(): total = lax.psum(total * jnp.exp(peak - highest), 'samples')  118 us
    reduce_sum x32, other arithmetic, accumulate(): jnp.sum(jnp.exp(logw - new_peak[None, :]), axis=0)  87 us
    psum x1, waiting for transfers between devices, local(): lax.psum((over, anchor, term_sum, weight_sum), 'samples')  59.8 us
    dot_general x8, matrix products, diagnose(): jnp.dot(weight.T, block, precision=lax.Precision.HIGHEST, preferred_eleme...  57.9 us
    reduce_sum x40, other arithmetic, denominator(): return top[:, 0] + jnp.log(jnp.sum(jnp.exp(shifted - top), axis=1))  54.4 us
    dot_general x8, matrix products, diagnose(): jnp.dot(weight.T, weight * scaled_counts[None, :], precision=lax.Precisio...  39 us
  transfers between devices with their start and end apart: 1, of which 1 were waited for; matrix products, arithmetic and copies ran while one was open for 0% of the time, Pallas kernels for 0%

commit v1 on v0

--- a/solution.py
+++ b/solution.py
@@ -1,6 +1,10 @@
+import functools
+
 import jax
 import jax.numpy as jnp
 from jax import lax
+from jax.experimental import pallas as pl
+from jax.experimental.pallas import tpu as pltpu
 from jax.sharding import PartitionSpec as P
 
 ITERS = 4
@@ -18,7 +22,7 @@
     return top[:, 0] + jnp.log(jnp.sum(jnp.exp(shifted - top), axis=1))
 
 
-def local(terms, coefficients, counts, labels, f_start):
+def general(terms, coefficients, counts, labels, f_start):
     rows = terms.shape[0]
     states = coefficients.shape[1]
     block_rows = min(4096, rows)
@@ -88,9 +92,400 @@
     return (free_now, over, anchor, term_sum / weight_sum[:, None])
 
 
+LOG2E = 1.4426950408889634
+LIFT = 57.0
+MESH = pl.DeviceIdType.MESH
+
+
+def lanes_to_column(rows_form):
+    parts = [
+        jnp.broadcast_to(rows_form[r : r + 1, :], (128, 128)).T for r in range(rows_form.shape[0])
+    ]
+    return jnp.concatenate(parts, axis=0)
+
+
+def split(x):
+    high = x.astype(jnp.bfloat16)
+    rest = x - high.astype(jnp.float32)
+    middle = rest.astype(jnp.bfloat16)
+    low = (rest - middle.astype(jnp.float32)).astype(jnp.bfloat16)
+    return high, middle, low
+
+
+def mbar_kernel(
+    n,
+    groups,
+    terms_ref,
+    coef_ref,
+    counts_ref,
+    labels_ref,
+    start_ref,
+    free_ref,
+    over_ref,
+    anchor_ref,
+    means_ref,
+    ok_ref,
+    q_ref,
+    t_ref,
+    a_ref,
+    w_ref,
+    d_ref,
+    acc_ref,
+    inv_ref,
+    x_ref,
+    left_ref,
+    right_ref,
+    comm_ref,
+    flag_ref,
+    big_ref,
+    half_ref,
+    red_ref,
+    got_ref,
+    load_sem,
+    send_sem,
+    recv_sem,
+    flag_send,
+    flag_recv,
+    half_sem,
+    out_send,
+    out_recv,
+):
+    f32, bf16 = jnp.float32, jnp.bfloat16
+    group = lax.axis_index("groups")
+    me = lax.axis_index("samples")
+    states = q_ref.shape[0]
+    rows = q_ref.shape[1]
+    terms = t_ref.shape[0]
+    owned = states // n
+    chunks = load_sem.shape[0]
+    chunk = rows // chunks
+
+    def load(c):
+        cols = pl.ds(pl.multiple_of(c * chunk, chunk), chunk)
+        return pltpu.make_async_copy(terms_ref.at[:, cols], t_ref.at[:, cols], load_sem.at[c])
+
+    barrier = pltpu.get_barrier_semaphore()
+    for d in range(1, n):
+        pl.semaphore_signal(
+            barrier, inc=1, device_id=(group, lax.rem(me + d, n)), device_id_type=MESH
+        )
+    for d in range(1, groups):
+        pl.semaphore_signal(
+            barrier, inc=1, device_id=(lax.rem(group + d, groups), me), device_id_type=MESH
+        )
+    for c in range(chunks):
+        load(c).start()
+
+    ch, cm, cl = (p.astype(f32) for p in split(coef_ref[...] * (-LOG2E)))
+    a_ref[...] = jnp.concatenate([ch, ch, cm, cm, ch, cl], axis=0).T.astype(bf16)
+
+    counts = counts_ref[...].astype(f32)
+    log_counts = jnp.log(counts)
+    tiny = 1e-15
+    most = 1e10
+
+    def state_weights(free):
+        shifted = log_counts + free
+        top = jnp.max(jnp.max(shifted, axis=1, keepdims=True), axis=0, keepdims=True)
+        return jnp.exp(shifted - top), top
+
+    def gather_sums(cols, width):
+        s = None
+        for k in range(0, states, 8):
+            w = w_ref[k : k + 8, :]
+            p = [q_ref[k : k + 8, pl.ds(cols + j, 128)] * w for j in range(0, width, 128)]
+            s = p if s is None else [x + y for x, y in zip(s, p)]
+        inv = [1.0 / jnp.sum(x, axis=0, keepdims=True) for x in s]
+        peak = functools.reduce(jnp.maximum, inv)
+        inv_ref[...] = jnp.maximum(inv_ref[...], peak)
+        wide = [jnp.broadcast_to(x, (8, 128)) for x in inv]
+        for k in range(0, states, 8):
+            t = [
+                q_ref[k : k + 8, pl.ds(cols + j, 128)] * wide[i]
+                for i, j in enumerate(range(0, width, 128))
+            ]
+            while len(t) > 1:
+                t = [t[i] + t[i + 1] for i in range(0, len(t), 2)]
+            acc_ref[k : k + 8, :] += t[0]
+
+    def clear():
+        acc_ref[...] = jnp.zeros_like(acc_ref)
+        inv_ref[...] = jnp.zeros_like(inv_ref)
+
+    weights, _ = state_weights(start_ref[...])
+    w_ref[...] = lanes_to_column(weights)
+    clear()
+
+    wa = WIDTH_A
+    wi = WIDTH_I
+
+    def energy_block(b, carry):
+        cols = pl.multiple_of(b * wa, wa)
+        th, tm, tl = split(t_ref[:, pl.ds(cols, wa)])
+        stacked = jnp.concatenate([th, tm, th, tm, tl, th], axis=0)
+        e = jnp.dot(a_ref[...], stacked, preferred_element_type=f32)
+        top = jnp.max(e, axis=0, keepdims=True) - LIFT
+        q_ref[:, pl.ds(cols, wa)] = jnp.exp2(e - top)
+        gather_sums(cols, wa)
+        return carry
+
+    def energy_chunk(c, carry):
+        load(c).wait()
+        per = chunk // wa
+        lax.fori_loop(c * per, (c + 1) * per, energy_block, 0)
+        return carry
+
+    lax.fori_loop(0, chunks, energy_chunk, 0)
+    pl.semaphore_wait(barrier, n - 1 + groups - 1)
+
+    good = counts > 0.0
+    free = None
+    for it in range(ITERS):
+        if it:
+            clear()
+
+            def pass_block(b, carry):
+                gather_sums(pl.multiple_of(b * wi, wi), wi)
+                return carry
+
+            lax.fori_loop(0, rows // wi, pass_block, 0)
+        sums = jnp.sum(acc_ref[...].T, axis=0, keepdims=True)
+        halves = [sums[:, r : r + 128] for r in range(0, states, 128)]
+        pad = comm_ref.shape[2] - len(halves)
+        comm_ref[it, me] = jnp.concatenate(halves + [inv_ref[...]] * pad, axis=0)
+        copies = []
+        for d in range(1, n):
+            copy = pltpu.make_async_remote_copy(
+                src_ref=comm_ref.at[it, me],
+                dst_ref=comm_ref.at[it, me],
+                send_sem=send_sem.at[it, d],
+                recv_sem=recv_sem.at[it, d],
+                device_id=(group, lax.rem(me + d, n)),
+                device_id_type=MESH,
+            )
+            copy.start()
+            copies.append(copy)
+        for copy in copies:
+            copy.wait()
+        everyone = comm_ref[it]
+        total = jnp.sum(everyone[:, : states // 128], axis=0)
+        peak = jnp.max(jnp.max(everyone, axis=0)[states // 128 :], axis=0, keepdims=True)
+        peak = jnp.max(peak, axis=1, keepdims=True)
+        good = good & (total >= tiny) & (peak <= most)
+        logs = jnp.log(total)
+        free = logs[0:1, 0:1] - logs
+        before = weights
+        weights, top = state_weights(free)
+        w_ref[...] = lanes_to_column(weights)
+    free_ref[...] = free
+
+    change = weights / before
+    least = jnp.min(jnp.min(change, axis=1, keepdims=True), axis=0, keepdims=True)
+    widest = jnp.max(jnp.max(change, axis=1, keepdims=True), axis=0, keepdims=True)
+    good = good & (weights >= 1e-30) & (peak <= most * least) & (total >= tiny * widest)
+    good = jnp.min(jnp.where(good, 1.0, 0.0), axis=0, keepdims=True)
+    good = jnp.broadcast_to(jnp.min(good, axis=1, keepdims=True), (8, 128))
+    flag_ref[group] = good
+    flags = []
+    for d in range(1, groups):
+        copy = pltpu.make_async_remote_copy(
+            src_ref=flag_ref.at[group],
+            dst_ref=flag_ref.at[group],
+            send_sem=flag_send.at[d],
+            recv_sem=flag_recv.at[d],
+            device_id=(lax.rem(group + d, groups), me),
+            device_id_type=MESH,
+        )
+        copy.start()
+        flags.append(copy)
+
+    d_ref[...] = lanes_to_column(jnp.exp(free - top))
+    left_ref[...] = jnp.zeros_like(left_ref)
+    right_ref[...] = jnp.zeros_like(right_ref)
+    wd = x_ref.shape[1]
+    sub = 512
+    base = 3 * states
+    x_ref[base + terms : base + terms + 16, :] = jnp.ones((16, wd), bf16)
+
+    def weights_block(b, carry):
+        cols = pl.multiple_of(b * wd, wd)
+        for o in range(0, wd, sub):
+            s = None
+            for k in range(0, states, 8):
+                w = w_ref[k : k + 8, :]
+                p = [q_ref[k : k + 8, pl.ds(cols + o + j, 128)] * w for j in range(0, sub, 128)]
+                s = p if s is None else [x + y for x, y in zip(s, p)]
+            inv = [1.0 / jnp.sum(x, axis=0, keepdims=True) for x in s]
+            wide = [jnp.broadcast_to(x, (16, 128)) for x in inv]
+            names = [
+                jnp.broadcast_to(labels_ref[:, pl.ds(cols + o + j, 128)], (16, 128))
+                for j in range(0, sub, 128)
+            ]
+            ids = lax.broadcasted_iota(jnp.int32, (16, 128), 0)
+            for k in range(0, states, 16):
+                scale = d_ref[k : k + 16, :]
+                for i, j in enumerate(range(0, sub, 128)):
+                    v = q_ref[k : k + 16, pl.ds(cols + o + j, 128)] * wide[i] * scale
+                    high = v.astype(bf16)
+                    x_ref[k : k + 16, o + j : o + j + 128] = high
+                    x_ref[states + k : states + k + 16, o + j : o + j + 128] = (
+                        v - high.astype(f32)
+                    ).astype(bf16)
+                    x_ref[2 * states + k : 2 * states + k + 16, o + j : o + j + 128] = jnp.where(
+                        names[i] == ids + k, 1.0, 0.0
+                    ).astype(bf16)
+            t = t_ref[:, pl.ds(cols + o, sub)]
+            th = t.astype(bf16)
+            x_ref[base : base + terms, o : o + sub] = th
+            x_ref[base + terms + 16 : base + 2 * terms + 16, o : o + sub] = (
+                t - th.astype(f32)
+            ).astype(bf16)
+        nt = (((1,), (1,)), ((), ()))
+        left_ref[...] += lax.dot_general(
+            x_ref[...], x_ref[0:states, :], nt, preferred_element_type=f32
+        )
+        right_ref[...] += lax.dot_general(
+            x_ref[2 * states : base + terms + 16, :],
+            x_ref[states : 2 * states, :],
+            nt,
+            preferred_element_type=f32,
+        )
+        return carry
+
+    lax.fori_loop(0, rows // wd, weights_block, 0)
+
+    cross = left_ref[states : 2 * states, :]
+    over = left_ref[0:states, :] + cross + cross.T
+    anchor = left_ref[2 * states : base, :] + right_ref[0:states, :]
+    sums = (
+        left_ref[base : base + terms, :]
+        + left_ref[base + terms + 16 : base + 2 * terms + 16, :]
+        + right_ref[states : states + terms, :]
+    )
+    mass = left_ref[base + terms : base + terms + 16, :] + right_ref[
+        states + terms : states + terms + 16, :
+    ]
+    fill = jnp.zeros((128 - terms - 16, states), f32)
+    sums = jnp.concatenate([sums, mass, fill], axis=0).T
+    for p in range(n):
+        own = slice(p * owned, (p + 1) * owned)
+        big_ref[p % 2, p // 2, :, 0:states] = over[own]
+        big_ref[p % 2, p // 2, :, states : 2 * states] = anchor[own]
+        big_ref[p % 2, p // 2, :, 2 * states :] = sums[own]
+
+    side = lax.rem(me, 2)
+    place = me // 2
+    pair = pltpu.make_async_remote_copy(
+        src_ref=big_ref.at[1 - side],
+        dst_ref=half_ref,
+        send_sem=half_sem.at[0],
+        recv_sem=half_sem.at[1],
+        device_id=(group, place * 2 + 1 - side),
+        device_id_type=MESH,
+    )
+    pair.start()
+    pair.wait()
+    red_ref[...] = big_ref[side] + half_ref[...]
+    copies = []
+    for d in range(1, n // 2):
+        there = lax.rem(place + d, n // 2)
+        copy = pltpu.make_async_remote_copy(
+            src_ref=red_ref.at[there],
+            dst_ref=got_ref.at[place],
+            send_sem=out_send.at[d],
+            recv_sem=out_recv.at[d],
+            device_id=(group, there * 2 + side),
+            device_id_type=MESH,
+        )
+        copy.start()
+        copies.append(copy)
+    got_ref[place] = red_ref[place]
+    for copy in copies:
+        copy.wait()
+    for copy in flags:
+        copy.wait()
+    ok_ref[...] = jnp.min(flag_ref[...], axis=0)
+    final = jnp.sum(got_ref[...], axis=0)
+    wide_counts = jnp.concatenate([counts[r : r + 1] for r in range(states // 128)], axis=1)
+    over_ref[...] = final[:, 0:states] * wide_counts
+    anchor_ref[...] = final[:, states : 2 * states]
+    tail = final[:, 2 * states :]
+    means_ref[...] = tail[:, 0:terms] / tail[:, terms : terms + 1]
+
+
+WIDTH_A = 512
+WIDTH_I = 1024
+WIDTH_D = 2048
+
+
+def local(n, groups, terms, coefficients, counts, labels, f_start):
+    rows, width = terms.shape
+    states = coefficients.shape[1]
+    f32, bf16 = jnp.float32, jnp.bfloat16
+    owned = states // n
+    chunks = 8
+    vmem = pl.BlockSpec(memory_space=pltpu.VMEM)
+    stacked = 3 * states + 2 * width + 16
+    block = (n // 2, owned, 2 * states + 128)
+    dma = pltpu.SemaphoreType.DMA
+    free, over, anchor, means, ok = pl.pallas_call(
+        functools.partial(mbar_kernel, n, groups),
+        out_shape=(
+            jax.ShapeDtypeStruct((states // 128, 128), f32),
+            jax.ShapeDtypeStruct((owned, states), f32),
+            jax.ShapeDtypeStruct((owned, states), f32),
+            jax.ShapeDtypeStruct((owned, width), f32),
+            jax.ShapeDtypeStruct((8, 128), f32),
+        ),
+        in_specs=[pl.BlockSpec(memory_space=pltpu.HBM), vmem, vmem, vmem, vmem],
+        out_specs=(vmem,) * 5,
+        scratch_shapes=[
+            pltpu.VMEM((states, rows), f32),
+            pltpu.VMEM((width, rows), f32),
+            pltpu.VMEM((states, 6 * width), bf16),
+            pltpu.VMEM((states, 128), f32),
+            pltpu.VMEM((states, 128), f32),
+            pltpu.VMEM((states, 128), f32),
+            pltpu.VMEM((1, 128), f32),
+            pltpu.VMEM((stacked, WIDTH_D), bf16),
+            pltpu.VMEM((stacked, states), f32),
+            pltpu.VMEM((states + width + 16, states), f32),
+            pltpu.VMEM((ITERS, n, 4, 128), f32),
+            pltpu.VMEM((groups, 8, 128), f32),
+            pltpu.VMEM((2,) + block, f32),
+            pltpu.VMEM(block, f32),
+            pltpu.VMEM(block, f32),
+            pltpu.VMEM(block, f32),
+            dma((chunks,)),
+            dma((ITERS, n)),
+            dma((ITERS, n)),
+            dma((groups,)),
+            dma((groups,)),
+            dma((2,)),
+            dma((n // 2,)),
+            dma((n // 2,)),
+        ],
+        compiler_params=pltpu.CompilerParams(
+            collective_id=0, has_side_effects=True, vmem_limit_bytes=62 * 1024 * 1024
+        ),
+    )(
+        terms.T,
+        coefficients,
+        counts.reshape(states // 128, 128),
+        labels.reshape(1, rows),
+        f_start.reshape(states // 128, 128),
+    )
+    fast = (free.reshape(states), over, anchor, means)
+    return lax.cond(
+        ok[0, 0] > 0.5,
+        lambda: fast,
+        lambda: general(terms, coefficients, counts, labels, f_start),
+    )
+
+
 def solution(mesh):
     return jax.shard_map(
-        local,
+        functools.partial(local, mesh.shape["samples"], mesh.shape["groups"]),
         mesh=mesh,
         in_specs=(
             P(("groups", "samples"), None),

time: 908 us -> 150 us (0.17); the launches traced: 898 us -> 149 us
  matrix products: 335 us -> 0 us
  blocking collectives: 271 us -> 0 us
  other arithmetic: 176 us -> 0 us
  Pallas kernels: 0 us -> 130 us
  waiting for transfers between devices: 59.8 us -> 0 us
  local copies, waits for them, and re-layouts: 38.3 us -> 4.22 us
    dot_general x64 -> x0, matrix products: 335 us -> none  [the longest x40 208 us: energies(): jnp.dot(block, coefficients, precision=lax.Precision.HIGHEST, preferred_e...]
    reduce_sum x80 -> x0, other arithmetic: 148 us -> none  [the longest x32 87 us: accumulate(): jnp.sum(jnp.exp(logw - new_peak[None, :]), axis=0)]
    psum x5 -> x0, blocking collectives: 148 us -> none  [the longest x4 118 us: local(): total = lax.psum(total * jnp.exp(peak - highest), 'samples')]
    pallas_call x0 -> x1, Pallas kernels: none -> 130 us  [local(): pl.pallas_call(functools.partial(mbar_kernel, n, groups), out_shape=(jax....]
    pmax x4 -> x0, blocking collectives: 123 us -> none  [local(): highest = lax.pmax(peak, 'samples')]
    psum x1 -> x0, waiting for transfers between devices: 59.8 us -> none  [local(): lax.psum((over, anchor, term_sum, weight_sum), 'samples')]
    reduce_max x32 -> x0, other arithmetic: 22.3 us -> none  [accumulate(): new_peak = jnp.maximum(peak, jnp.max(logw, axis=0))]
    while x129 -> x0, local copies, waits for them, and re-layouts: 22.3 us -> none
  transfers between devices with their start and end apart: 1 -> 0, of which waited for: 1 -> 0; matrix products, arithmetic and copies ran while one was open for 0% -> 0% of each run, Pallas kernels for 0% -> 0%
where the time goes in v1:
time: 150 us; the launch traced here: 149 us
  Pallas kernels  130 us (87%)
  between operations  14.7 us (10%)
  local copies, waits for them, and re-layouts  4.22 us (3%)
    pallas_call x1, Pallas kernels, local(): pl.pallas_call(functools.partial(mbar_kernel, n, groups), out_shape=(jax....  130 us
    unnamed x12, local copies, waits for them, and re-layouts  3.02 us

profile of v1, /device:TPU:0, one launch (start us, length us, event | category | flops | bytes accessed | tf_op | source)
XLA Modules:
  0.0 149.4 jit_solution(12202248991441269677)
XLA Ops:
  7.2 0.0 copy-start.6
  7.2 0.0 copy-start.8
  7.2 0.0 copy-start.11
  7.2 0.0 copy-start.12
  7.2 130.2 %shard_map.92 = (f32[2,128]{1,0:T(2,128)}, f32[16,256]{1,0:T(8,128)S(1)}, f32[16,256]{1,0:T(8,128)S(1)}, f32[16,64]{1,0:T(8,128)S(1)}, f32[8,128]{1,0:T(8,128)}) custom-call(f32[64,32768]{1,0:T(8,128)} %bitcast.91, f32[64,256]{1,0:T(8,128)} %coef_ref.1, s32[2,128]{1,0:T(2,128)} %bitcast.109, s32[1,32768]{1,0:T(1,128)} %bitcast.92, f32[2,128]{1,0:T(2,128)} %bitcast.110), custom_call_target="tpu_custom_call" | custom-call | tf_op jit(solution)/shard_map/pallas_call | solution.py:431
  137.4 1.2 slice.15
  139.3 0.0 copy-done.6
  139.3 0.0 copy-done.8
  139.3 0.0 copy-done.11
  139.3 0.0 copy-done.12
  139.3 0.2 conditional.1
  139.5 1.2 copy.88
  140.7 0.6 copy.89
  141.3 0.6 copy.90
  141.9 0.6 copy.91
Async XLA Ops:
  7.2 132.1 %copy-start.6 = (f32[64,256]{1,0:T(8,128)S(1)}, f32[64,256]{1,0:T(8,128)}, u32[]{:S(2)}) copy-start(f32[64,256]{1,0:T(8,128)} %coef_ref.1) | copy-start | bytes 196612
  7.2 132.1 %copy-start.8 = (s32[32768]{0:T(1024)S(1)}, s32[32768]{0:T(1024)}, u32[]{:S(2)}) copy-start(s32[32768]{0:T(1024)} %param.20) | copy-start | bytes 393220
  7.2 132.1 %copy-start.11 = (s32[256]{0:T(256)S(1)}, s32[256]{0:T(256)}, u32[]{:S(2)}) copy-start(s32[256]{0:T(256)} %param.19) | copy-start | bytes 3076
  7.2 132.1 %copy-start.12 = (f32[256]{0:T(256)S(1)}, f32[256]{0:T(256)}, u32[]{:S(2)}) copy-start(f32[256]{0:T(256)} %param.21) | copy-start | bytes 3076

commit v2 on v1

--- a/solution.py
+++ b/solution.py
@@ -20,6 +20,20 @@
     shifted = log_counts[None, :] + free_now[None, :] - energy
     top = jnp.max(shifted, axis=1, keepdims=True)
     return top[:, 0] + jnp.log(jnp.sum(jnp.exp(shifted - top), axis=1))
+
+
+def from_all(x):
+    n = lax.axis_size("samples")
+    me = lax.axis_index("samples")
+    ring = [(i, (i + 1) % n) for i in range(n)]
+
+    def step(d, carry):
+        moving, held = carry
+        moving = lax.ppermute(moving, "samples", ring)
+        return moving, lax.dynamic_update_index_in_dim(held, moving, lax.rem(me - d + n, n), 0)
+
+    held = lax.dynamic_update_index_in_dim(jnp.zeros((n,) + x.shape, x.dtype), x, me, 0)
+    return lax.fori_loop(1, n, step, (x, held))[1]
 
 
 def general(terms, coefficients, counts, labels, f_start):
@@ -30,8 +44,7 @@
     label_blocks = labels.reshape(rows // block_rows, block_rows)
     log_counts = jnp.log(counts.astype(jnp.float32))
     scaled_counts = counts.astype(jnp.float32)
-    free_now = f_start
-    for step in range(ITERS):
+    def iterate(step, free_now):
 
         def accumulate(carry, block):
             peak, total = carry
@@ -46,11 +59,13 @@
 
         init = (jnp.full((states,), -1e30, jnp.float32), jnp.zeros((states,), jnp.float32))
         (peak, total), _ = lax.scan(accumulate, init, blocks)
-        highest = lax.pmax(peak, "samples")
-        total = lax.psum(total * jnp.exp(peak - highest), "samples")
+        highest = jnp.max(from_all(peak), axis=0)
+        total = jnp.sum(from_all(total * jnp.exp(peak - highest)), axis=0)
         peak = highest
         updated = -(peak + jnp.log(total))
-        free_now = updated - updated[0]
+        return updated - updated[0]
+
+    free_now = lax.fori_loop(0, ITERS, iterate, f_start)
     state_ids = jnp.arange(states, dtype=jnp.int32)
 
     def diagnose(carry, pair):
@@ -82,7 +97,9 @@
         jnp.zeros((states,), jnp.float32),
     )
     (over, anchor, term_sum, weight_sum), _ = lax.scan(diagnose, init, (blocks, label_blocks))
-    over, anchor, term_sum, weight_sum = lax.psum((over, anchor, term_sum, weight_sum), "samples")
+    over, anchor, term_sum, weight_sum = (
+        jnp.sum(from_all(x), axis=0) for x in (over, anchor, term_sum, weight_sum)
+    )
     owned = states // lax.axis_size("samples")
     first_row = lax.axis_index("samples") * owned
     over = lax.dynamic_slice_in_dim(over, first_row, owned, 0)
@@ -153,8 +170,8 @@
     f32, bf16 = jnp.float32, jnp.bfloat16
     group = lax.axis_index("groups")
     me = lax.axis_index("samples")
-    states = q_ref.shape[0]
-    rows = q_ref.shape[1]
+    blocks, states, wq = q_ref.shape
+    rows = blocks * wq
     terms = t_ref.shape[0]
     owned = states // n
     chunks = load_sem.shape[0]
@@ -189,21 +206,23 @@
         top = jnp.max(jnp.max(shifted, axis=1, keepdims=True), axis=0, keepdims=True)
         return jnp.exp(shifted - top), top
 
-    def gather_sums(cols, width):
+    def gather_sums(block, count):
+        lanes = [(c, j) for c in range(count) for j in range(0, wq, 128)]
+
+        def tile(k, c, j):
+            return q_ref[block + c, k : k + 8, j : j + 128]
+
         s = None
         for k in range(0, states, 8):
             w = w_ref[k : k + 8, :]
-            p = [q_ref[k : k + 8, pl.ds(cols + j, 128)] * w for j in range(0, width, 128)]
+            p = [tile(k, c, j) * w for c, j in lanes]
             s = p if s is None else [x + y for x, y in zip(s, p)]
         inv = [1.0 / jnp.sum(x, axis=0, keepdims=True) for x in s]
         peak = functools.reduce(jnp.maximum, inv)
         inv_ref[...] = jnp.maximum(inv_ref[...], peak)
         wide = [jnp.broadcast_to(x, (8, 128)) for x in inv]
         for k in range(0, states, 8):
-            t = [
-                q_ref[k : k + 8, pl.ds(cols + j, 128)] * wide[i]
-                for i, j in enumerate(range(0, width, 128))
-            ]
+            t = [tile(k, c, j) * wide[i] for i, (c, j) in enumerate(lanes)]
             while len(t) > 1:
                 t = [t[i] + t[i + 1] for i in range(0, len(t), 2)]
             acc_ref[k : k + 8, :] += t[0]
@@ -216,22 +235,24 @@
     w_ref[...] = lanes_to_column(weights)
     clear()
 
-    wa = WIDTH_A
-    wi = WIDTH_I
-
-    def energy_block(b, carry):
-        cols = pl.multiple_of(b * wa, wa)
-        th, tm, tl = split(t_ref[:, pl.ds(cols, wa)])
+    def energies_of(b):
+        cols = pl.multiple_of(b * wq, wq)
+        th, tm, tl = split(t_ref[:, pl.ds(cols, wq)])
         stacked = jnp.concatenate([th, tm, th, tm, tl, th], axis=0)
-        e = jnp.dot(a_ref[...], stacked, preferred_element_type=f32)
-        top = jnp.max(e, axis=0, keepdims=True) - LIFT
-        q_ref[:, pl.ds(cols, wa)] = jnp.exp2(e - top)
-        gather_sums(cols, wa)
+        return jnp.dot(a_ref[...], stacked, preferred_element_type=f32)
+
+    def energy_block(i, carry):
+        b = i * 2
+        es = [energies_of(b), energies_of(b + 1)]
+        for c, e in enumerate(es):
+            top = jnp.max(e, axis=0, keepdims=True) - LIFT
+            q_ref[b + c] = jnp.exp2(e - top)
+        gather_sums(b, 2)
         return carry
 
     def energy_chunk(c, carry):
         load(c).wait()
-        per = chunk // wa
+        per = chunk // (2 * wq)
         lax.fori_loop(c * per, (c + 1) * per, energy_block, 0)
         return carry
 
@@ -245,10 +266,10 @@
             clear()
 
             def pass_block(b, carry):
-                gather_sums(pl.multiple_of(b * wi, wi), wi)
+                gather_sums(b * 2, 2)
                 return carry
 
-            lax.fori_loop(0, rows // wi, pass_block, 0)
+            lax.fori_loop(0, blocks // 2, pass_block, 0)
         sums = jnp.sum(acc_ref[...].T, axis=0, keepdims=True)
         halves = [sums[:, r : r + 128] for r in range(0, states, 128)]
         pad = comm_ref.shape[2] - len(halves)
@@ -303,17 +324,19 @@
     left_ref[...] = jnp.zeros_like(left_ref)
     right_ref[...] = jnp.zeros_like(right_ref)
     wd = x_ref.shape[1]
-    sub = 512
+    sub = wq
     base = 3 * states
     x_ref[base + terms : base + terms + 16, :] = jnp.ones((16, wd), bf16)
 
     def weights_block(b, carry):
         cols = pl.multiple_of(b * wd, wd)
-        for o in range(0, wd, sub):
+        for u in range(wd // sub):
+            o = u * sub
+            at = b * (wd // sub) + u
             s = None
             for k in range(0, states, 8):
                 w = w_ref[k : k + 8, :]
-                p = [q_ref[k : k + 8, pl.ds(cols + o + j, 128)] * w for j in range(0, sub, 128)]
+                p = [q_ref[at, k : k + 8, j : j + 128] * w for j in range(0, sub, 128)]
                 s = p if s is None else [x + y for x, y in zip(s, p)]
             inv = [1.0 / jnp.sum(x, axis=0, keepdims=True) for x in s]
             wide = [jnp.broadcast_to(x, (16, 128)) for x in inv]
@@ -325,7 +348,7 @@
             for k in range(0, states, 16):
                 scale = d_ref[k : k + 16, :]
                 for i, j in enumerate(range(0, sub, 128)):
-                    v = q_ref[k : k + 16, pl.ds(cols + o + j, 128)] * wide[i] * scale
+                    v = q_ref[at, k : k + 16, j : j + 128] * wide[i] * scale
                     high = v.astype(bf16)
                     x_ref[k : k + 16, o + j : o + j + 128] = high
                     x_ref[states + k : states + k + 16, o + j : o + j + 128] = (
@@ -413,8 +436,7 @@
     means_ref[...] = tail[:, 0:terms] / tail[:, terms : terms + 1]
 
 
-WIDTH_A = 512
-WIDTH_I = 1024
+WIDTH_Q = 512
 WIDTH_D = 2048
 
 
@@ -440,7 +462,7 @@
         in_specs=[pl.BlockSpec(memory_space=pltpu.HBM), vmem, vmem, vmem, vmem],
         out_specs=(vmem,) * 5,
         scratch_shapes=[
-            pltpu.VMEM((states, rows), f32),
+            pltpu.VMEM((rows // WIDTH_Q, states, WIDTH_Q), f32),
             pltpu.VMEM((width, rows), f32),
             pltpu.VMEM((states, 6 * width), bf16),
             pltpu.VMEM((states, 128), f32),

time: 150 us -> 107 us (0.71)
  Pallas kernels: 130 us -> 102 us
  between operations: 14.7 us -> 1.34 us
    pallas_call x1, Pallas kernels: 130 us -> 102 us  [local(): pl.pallas_call(functools.partial(mbar_kernel, n, groups), out_shape=(jax....]
where the time goes in v2:
time: 107 us
  Pallas kernels  102 us (95%)
  local copies, waits for them, and re-layouts  3.71 us (3%)
  between operations  1.34 us (1%)
    pallas_call x1, Pallas kernels, local(): pl.pallas_call(functools.partial(mbar_kernel, n, groups), out_shape=(jax....  102 us
    unnamed x12, local copies, waits for them, and re-layouts  2.51 us

profile of v2, /device:TPU:0, one launch (start us, length us, event | category | flops | bytes accessed | tf_op | source)
XLA Modules:
  0.0 107.2 jit_solution(10468837716067516140)
XLA Ops:
  0.6 0.7 copy.133
  1.3 0.0 copy-start.3
  1.3 0.0 copy-start.4
  1.3 0.0 copy-start.6
  1.3 102.0 %shard_map.90 = (f32[2,128]{1,0:T(2,128)S(1)}, f32[16,256]{1,0:T(8,128)S(1)}, f32[16,256]{1,0:T(8,128)S(1)}, f32[16,64]{1,0:T(8,128)S(1)}, f32[8,128]{1,0:T(8,128)}) custom-call(f32[64,32768]{1,0:T(8,128)} %bitcast.83, f32[64,256]{1,0:T(8,128)} %coef_ref.1, s32[2,128]{1,0:T(2,128)} %bitcast.100, s32[1,32768]{1,0:T(1,128)} %bitcast.91, f32[2,128]{1,0:T(2,128)S(1)} %bitcast.93), custom_call_target="tpu_custom_call" | custom-call | tf_op jit(solution)/shard_map/pallas_call | solution.py:453
  103.3 1.2 %slice.6 = f32[1,1]{1,0:T(1,128)} slice(f32[8,128]{1,0:T(8,128)} %get-tuple-element.765), slice={[0:1], [0:1]} | slice | bytes 8 | tf_op jit(solution)/shard_map/slice | solution.py:502
  105.1 0.0 copy-done.3
  105.1 0.0 copy-done.4
  105.2 0.0 copy-done.6
  105.2 0.2 conditional.1
  105.4 0.0 copy-start.5
  105.4 0.6 copy.135
  106.0 0.6 copy.136
  106.6 0.6 copy.137
  107.2 0.0 copy-done.5
  (1 shorter events, 0.0 us)
Async XLA Ops:
  1.3 103.8 %copy-start.3 = (f32[64,256]{1,0:T(8,128)S(1)}, f32[64,256]{1,0:T(8,128)}, u32[]{:S(2)}) copy-start(f32[64,256]{1,0:T(8,128)} %coef_ref.1) | copy-start | bytes 196612
  1.3 103.8 %copy-start.4 = (s32[32768]{0:T(1024)S(1)}, s32[32768]{0:T(1024)}, u32[]{:S(2)}) copy-start(s32[32768]{0:T(1024)} %param.28) | copy-start | bytes 393220
  1.3 103.8 %copy-start.6 = (s32[256]{0:T(256)S(1)}, s32[256]{0:T(256)}, u32[]{:S(2)}) copy-start(s32[256]{0:T(256)} %param.27) | copy-start | bytes 3076
  105.4 1.8 %copy-start.5 = (f32[256]{0:T(256)}, f32[256]{0:T(256)S(1)}, u32[]{:S(2)}) copy-start(f32[256]{0:T(256)S(1)} %get-tuple-element.1551) | copy-start | bytes 3076
